TPU v7x, 32 devices: a whole 2x2x4 slice. The times are simulated.
32 devices in a mesh: dp: 8 (over z, x), mp: 4 (over y, core).
Axes of the slice: x: 2, y: 2, z: 4, core: 2. Of those that a mesh axis runs over, the one named last changes fastest.
Arguments:
- vision: bfloat16 [2048, 3200], P(('dp', 'mp')), may hold values from -6 to 6
- vision_gain: float32 [3200], replicated, may hold values from 0.1 to 1.9
- image_slot: int32 [8], replicated, may hold values from 0 to 15, as said below
- text_embed: bfloat16 [4096, 8192], P('dp', 'mp'), may hold values from -6 to 6
- w_proj: bfloat16 [3200, 8192], P(None, 'mp'), may hold values from -0.109375 to 0.109375
- llm_gain: float32 [8192], P('mp'), may hold values from 0.1 to 1.9
- w_key: bfloat16 [8192, 1024], P('mp'), may hold values from -0.0625 to 0.0625
- w_value: bfloat16 [8192, 1024], P('mp'), may hold values from -0.0625 to 0.0625
- key_grad: bfloat16 [4096, 1024], P('dp', 'mp'), may hold values from -6 to 6
- value_grad: bfloat16 [4096, 1024], P('dp', 'mp'), may hold values from -6 to 6
Outputs:
- key_out: bfloat16 [4096, 1024], P('dp', 'mp')
- value_out: bfloat16 [4096, 1024], P('dp', 'mp')
- text_grad: bfloat16 [4096, 8192], P('dp', 'mp')
- vision_grad: bfloat16 [2048, 3200], P(('dp', 'mp'))
Inputs may be any that keep to these rules, and one draw needn't show every extreme that they name: `image_slot`: the 8 entries are different slots. Image i is encoded on index i of dp; slot j covers positions j * 256 to (j + 1) * 256 - 1, so it lies on index j // 2 of dp. One index of dp receives 2 images, every other one at most one.
All inputs are finite; a program needn't handle non-finite values.
Results may differ from a plain program's by a relative error of at most 0.0058.
Values may be sent and summed in bfloat16 or wider, within the bound.
A program may use at most 128 MiB of HBM per device.

v0:
```python
import jax
import jax.numpy as jnp
from jax import lax
from jax.sharding import PartitionSpec as P

D = 8192
PATCH = 256


def shards(
    vision,
    vision_gain,
    image_slot,
    text_embed,
    w_proj,
    llm_gain,
    w_key,
    w_value,
    key_grad,
    value_grad,
):
    dp_count = lax.axis_size("dp")
    here = lax.axis_index("dp")
    slot_dev = text_embed.shape[0] // PATCH
    img_rows = vision.shape[0]
    width_dev = text_embed.shape[1]
    vision_f = vision.astype(jnp.float32)
    vis_scale = lax.rsqrt(jnp.mean(vision_f * vision_f, axis=1, keepdims=True) + 1e-06)
    vis_normed = (vision_f * vis_scale * vision_gain).astype(jnp.bfloat16)
    sources = jnp.arange(dp_count, dtype=jnp.int32)
    dest_all = image_slot // slot_dev
    within_all = image_slot % slot_dev
    mine = dest_all == here
    pick_mask = (within_all[None, :] == jnp.arange(slot_dev, dtype=jnp.int32)[:, None]) & mine[
        None, :
    ]
    pick = pick_mask.astype(jnp.bfloat16)
    filled = jnp.sum(pick_mask.astype(jnp.float32), axis=1) > 0.5
    my_dest = jnp.sum(jnp.where(sources == here, dest_all, 0))
    dest_hot = sources == my_dest
    slot_ids = jnp.arange(dp_count * slot_dev, dtype=jnp.int32)
    slot_pick = (slot_ids[:, None] == image_slot[None, :]).astype(jnp.bfloat16)
    outbox = jnp.where(dest_hot[:, None, None], vis_normed[None], jnp.zeros_like(vis_normed)[None])
    inbox = lax.all_to_all(outbox, "dp", split_axis=0, concat_axis=0, tiled=True)
    arrived = jnp.einsum("ks,srv->krv", pick, inbox, preferred_element_type=jnp.float32).astype(
        jnp.bfloat16
    )
    image_embed = jnp.einsum(
        "srv,vd->srd",
        lax.all_gather(arrived, "mp", axis=1, tiled=True),
        w_proj,
        preferred_element_type=jnp.float32,
    ).astype(jnp.bfloat16)
    text_blocks = text_embed.reshape(slot_dev, PATCH, width_dev)
    embed = jnp.where(filled[:, None, None], image_embed, text_blocks).reshape(
        slot_dev * PATCH, width_dev
    )
    embed_f = embed.astype(jnp.float32)
    square_total = lax.psum(jnp.sum(embed_f * embed_f, axis=1), "mp")
    scale = lax.rsqrt(square_total / D + 1e-05)[:, None]
    llm_normed = (embed_f * scale * llm_gain).astype(jnp.bfloat16)
    key_part = jnp.dot(llm_normed, w_key, preferred_element_type=jnp.float32)
    value_part = jnp.dot(llm_normed, w_value, preferred_element_type=jnp.float32)
    key_sum, value_sum = (
        lax.psum_scatter(key_part, "mp", scatter_dimension=1, tiled=True),
        lax.psum_scatter(value_part, "mp", scatter_dimension=1, tiled=True),
    )
    key_out = key_sum.astype(jnp.bfloat16)
    value_out = value_sum.astype(jnp.bfloat16)
    stacked = jnp.stack([key_grad, value_grad])
    piece = lax.all_gather(stacked, "mp", axis=2, tiled=True)
    contract = (((1,), (1,)), ((), ()))
    carry = lax.dot_general(piece[0], w_key, contract, preferred_element_type=jnp.float32)
    d_normed = carry + lax.dot_general(
        piece[1], w_value, contract, preferred_element_type=jnp.float32
    )
    grad_g = d_normed * llm_gain
    inner_total = lax.psum(jnp.sum(grad_g * embed_f, axis=1), "mp")
    d_embed = scale * grad_g - embed_f * scale * scale * scale * (inner_total / D)[:, None]
    d_blocks = d_embed.reshape(slot_dev, PATCH, width_dev)
    text_grad = (
        jnp.where(filled[:, None, None], 0.0, d_blocks)
        .reshape(slot_dev * PATCH, width_dev)
        .astype(jnp.bfloat16)
    )
    image_grad = d_blocks.astype(jnp.bfloat16)
    piece = image_grad
    d_vis_rows = lax.psum_scatter(
        jnp.einsum("srd,vd->rsv", piece, w_proj, preferred_element_type=jnp.float32),
        "mp",
        scatter_dimension=0,
        tiled=True,
    )
    d_vis_slots = jnp.transpose(d_vis_rows, (1, 0, 2)).astype(jnp.bfloat16)
    spread_back = lax.all_to_all(d_vis_slots[None], "dp", split_axis=3, concat_axis=0, tiled=True)
    spread_back = spread_back.reshape(dp_count * slot_dev, img_rows, spread_back.shape[3])
    per_image = jnp.einsum(
        "ji,jrc->irc", slot_pick, spread_back, preferred_element_type=jnp.float32
    ).astype(jnp.bfloat16)
    d_vis = lax.all_to_all(per_image, "dp", split_axis=0, concat_axis=2, tiled=True)[0].astype(
        jnp.float32
    )
    grad_h = d_vis * vision_gain
    vis_inner = jnp.mean(grad_h * vision_f, axis=1, keepdims=True)
    vision_grad = vis_scale * grad_h - vision_f * vis_scale * vis_scale * vis_scale * vis_inner
    return (key_out, value_out, text_grad, vision_grad.astype(jnp.bfloat16))


def solution(mesh):
    placed = (
        P(("dp", "mp"), None),
        P(),
        P(),
        P("dp", "mp"),
        P(None, "mp"),
        P("mp"),
        P("mp", None),
        P("mp", None),
        P("dp", "mp"),
        P("dp", "mp"),
    )
    return jax.shard_map(
        shards,
        mesh=mesh,
        in_specs=placed,
        out_specs=(P("dp", "mp"), P("dp", "mp"), P("dp", "mp"), P(("dp", "mp"), None)),
        check_vma=False,
    )
```

profile of v0, /device:TPU:0, one launch (start us, length us, event | category | flops | bytes accessed | tf_op | source)
XLA Modules:
  0.0 306.5 jit_solution(563517451565397470)
XLA Ops:
  7.2 1.2 fusion.35
  11.5 2.1 broadcast_select_fusion
  13.6 7.4 %all-to-all-start = ((bf16[8,64,3200]{2,1,0:T(8,128)(2,1)}), bf16[8,64,3200]{2,1,0:T(8,128)(2,1)S(1)}, u32[]{:S(2)}, u32[]{:S(2)}) async-start(bf16[8,64,3200]{2,1,0:T(8,128)(2,1)} %broadcast_select_fusion), calls=%async_computation | async-start | bytes 6553600 | tf_op jit(solution)/shard_map/all_to_all | solution.py:44
  21.0 1.8 pad_maximum_fusion
  22.9 71.5 %all-to-all-done = bf16[8,64,3200]{2,1,0:T(8,128)(2,1)S(1)} async-done(((bf16[8,64,3200]{2,1,0:T(8,128)(2,1)}), bf16[8,64,3200]{2,1,0:T(8,128)(2,1)S(1)}, u32[]{:S(2)}, u32[]{:S(2)}) %all-to-all-start) | async-done | bytes 3276832 | tf_op jit(solution)/shard_map/all_to_all | solution.py:44
  94.5 3.9 %convolution_convert_fusion = bf16[2,64,3200]{2,0,1:T(2,128)(2,1)} fusion(bf16[8,64,3200]{2,1,0:T(8,128)(2,1)S(1)} %all-to-all-done, pred[8]{0:T(512)(128)(4,1)S(1)} %get-tuple-element.6, s32[8]{0:T(128)S(1)} %and_select_fusion.1), kind=kOutput, calls=%fused_computation.5 | convolution fusion | flops 6963232 | bytes 4096040 | tf_op jit(solution)/shard_map/ks,srv->krv/dot_general | solution.py:45
  98.7 7.0 %fusion.27 = f32[512,2048]{1,0:T(8,128)} fusion(bf16[2048,1024]{1,0:T(8,128)(2,1)} %param.16, bf16[2,512,1024]{2,1,0:T(8,128)(2,1)} %all-gather.5.cloned.1.call-done), kind=kOutput, calls=%fused_computation.30 | convolution fusion | flops 2147483648 | bytes 9437184 | tf_op jit(solution)/shard_map/dot_general | solution.py:73
  105.7 21.2 %all-gather.3.cloned.1.call-done = bf16[2,256,3200]{2,0,1:T(2,128)(2,1)} async-done(((bf16[2,64,3200]{2,0,1:T(2,128)(2,1)}), bf16[2,256,3200]{2,0,1:T(2,128)(2,1)}) %all-gather.3.cloned.1.call-update) | async-done | bytes 3276816 | tf_op jit(solution)/shard_map/all_gather | solution.py:50
  126.9 11.6 %fusion.13 = (f32[2,256]{1,0:T(2,128)S(1)}, bf16[2,256,2048]{2,1,0:T(8,128)(2,1)S(1)}) fusion(bf16[2,256,2048]{2,1,0:T(8,128)(2,1)S(1)} %bitcast.89, bf16[3200,2048]{1,0:T(8,128)(2,1)} %param.14, bf16[2,256,3200]{2,0,1:T(2,128)(2,1)} %all-gather.3.cloned.1.call-done, pred[2]{0:T(512)(128)(4,1)S(1)} %broadcast_compare_fusion), kind=kOutput, calls=%fused_computation.15 | convolution fusion | flops 6716128768 | bytes 20580354 | tf_op jit(solution)/shard_map/srv,vd->srd/dot_general | solution.py:48
  138.6 4.7 %fusion.14 = (f32[512]{0:T(512)S(1)}, f32[512,2048]{1,0:T(8,128)}) fusion(bf16[2,256,2048]{2,1,0:T(8,128)(2,1)S(1)} %get-tuple-element.12, f32[2048]{0:T(1024)S(1)} %copy-done.4, f32[512,2048]{1,0:T(8,128)S(1)} %copy-done.9, bf16[2048,1024]{1,0:T(8,128)(2,1)S(1)} %copy-done.6, bf16[2,512,1024]{2,1,0:T(8,128)(2,1)S(1)} %copy-done.8), kind=kOutput, calls=%fused_computation.16 | convolution fusion | flops 2152726016 | bytes 15738880 | tf_op jit(solution)/shard_map/dot_general | solution.py:74
  143.3 6.0 %all-reduce = (f32[512]{0:T(512)S(1)}, f32[512]{0:T(512)S(1)}) all-reduce(f32[512]{0:T(512)S(1)} %bitcast.87, f32[512]{0:T(512)S(1)} %get-tuple-element.13), channel_id=1, replica_groups=mesh['dp'=8,'mp'=4] {'mp'}, use_global_device_ids=true, to_apply=%region_4.5 | all-reduce | flops 1024 | bytes 8192 | tf_op jit(solution)/shard_map/psum | solution.py:59
  149.3 4.7 %fusion.44 = (bf16[512,2048]{1,0:T(8,128)(2,1)S(1)}, bf16[512,2048]{1,0:T(8,128)(2,1)}, bf16[512,2048]{1,0:T(8,128)(2,1)S(1)}) fusion(f32[512]{0:T(512)S(1)} %get-tuple-element.16, bf16[2,256,2048]{2,1,0:T(8,128)(2,1)} %copy-done.1, f32[512,2048]{1,0:T(8,128)} %get-tuple-element.14, f32[512]{0:T(512)S(1)} %get-tuple-element.15, ...), kind=kLoop, calls=%fused_computation.65 | loop fusion | flops 12582912 | bytes 12595712 | tf_op jit(solution)/shard_map/convert_element_type | solution.py:86
  154.0 12.6 %fusion.4 = f32[256,2,3200]{2,0,1:T(8,128)} fusion(bf16[2,256,2048]{2,1,0:T(8,128)(2,1)S(1)} %bitcast.84, bf16[3200,2048]{1,0:T(8,128)(2,1)} %param.14), kind=kOutput, calls=%fused_computation.4 | convolution fusion | flops 6710886400 | bytes 21757952 | tf_op jit(solution)/shard_map/srd,vd->rsv/dot_general | solution.py:89
  166.7 5.9 %fusion.45 = f32[512,1024]{1,0:T(8,128)} fusion(bf16[512,2048]{1,0:T(8,128)(2,1)S(1)} %get-tuple-element.10, bf16[2048,1024]{1,0:T(8,128)(2,1)} %param.16), kind=kOutput, calls=%fused_computation.66 | convolution fusion | flops 2147483648 | bytes 8388608 | tf_op jit(solution)/shard_map/dot_general | solution.py:62
  172.7 6.6 %fusion.46 = f32[512,1024]{1,0:T(8,128)} fusion(bf16[512,2048]{1,0:T(8,128)(2,1)S(1)} %get-tuple-element.10, bf16[2048,1024]{1,0:T(8,128)(2,1)} %param.17), kind=kOutput, calls=%fused_computation.67 | convolution fusion | flops 2147483648 | bytes 8388608 | tf_op jit(solution)/shard_map/dot_general | solution.py:63
  179.3 49.2 %reduce-scatter.8.cloned.1.call-done = f32[64,2,3200]{2,0,1:T(8,128)} async-done(((f32[256,2,3200]{2,0,1:T(8,128)}), f32[64,2,3200]{2,0,1:T(8,128)}) %reduce-scatter.8.cloned.1.call-update) | async-done | bytes 1638416 | tf_op jit(solution)/shard_map/reduce_scatter | solution.py:88
  228.5 1.5 convert_bitcast_fusion.1
  230.0 1.2 copy.25
  232.3 26.8 %all_to_all.29 = bf16[8,2,25600]{2,1,0:T(2,128)(2,1)S(1)} all-to-all(bf16[8,2,25600]{2,1,0:T(2,128)(2,1)S(1)} %reshape.63), channel_id=1, replica_groups=mesh['dp'=8,'mp'=4] {'dp'}, dimensions={0} | all-to-all | bytes 1638400 | tf_op jit(solution)/shard_map/all_to_all | solution.py:95
  260.0 1.7 copy.26
  263.9 3.5 %all-to-all-start.2 = ((bf16[8,64,400]{2,1,0:T(8,128)(2,1)}), bf16[8,64,400]{2,1,0:T(8,128)(2,1)S(1)}, u32[]{:S(2)}, u32[]{:S(2)}) async-start(bf16[8,64,400]{2,1,0:T(8,128)(2,1)} %copy.27), calls=%async_computation.5 | async-start | bytes 1048576 | tf_op jit(solution)/shard_map/all_to_all | solution.py:100
  267.4 1.8 convert_element_type.77
  269.2 26.5 %reduce-scatter.6.cloned.1.call-done = f32[512,256]{1,0:T(8,128)} async-done(((f32[512,1024]{1,0:T(8,128)}), f32[512,256]{1,0:T(8,128)}) %reduce-scatter.6.cloned.1.call-update) | async-done | bytes 524304 | tf_op jit(solution)/shard_map/reduce_scatter | solution.py:66
  295.7 1.8 convert_element_type.78
  (56 shorter events, 10.4 us)
Async XLA Ops:
  13.6 7.5 %copy-start.2 = (bf16[512,256]{1,0:T(8,128)(2,1)S(1)}, bf16[512,256]{1,0:T(8,128)(2,1)}, u32[]{:S(2)}) copy-start(bf16[512,256]{1,0:T(8,128)(2,1)} %param.19) | copy-start | bytes 786436
  13.6 9.4 %copy-start.5 = (s32[8]{0:T(128)S(1)}, s32[8]{0:T(128)}, u32[]{:S(2)}) copy-start(s32[8]{0:T(128)} %param.12) | copy-start | bytes 100
  13.6 80.9 %all-to-all-start = ((bf16[8,64,3200]{2,1,0:T(8,128)(2,1)}), bf16[8,64,3200]{2,1,0:T(8,128)(2,1)S(1)}, u32[]{:S(2)}, u32[]{:S(2)}) async-start(bf16[8,64,3200]{2,1,0:T(8,128)(2,1)} %broadcast_select_fusion), calls=%async_computation | async-start | bytes 6553600 | tf_op jit(solution)/shard_map/all_to_all | solution.py:44
  21.0 77.7 %all-gather.5.cloned.1.call-start = ((), (), s32[]{:S(2)}) async-start(), calls=%async_computation.9 | async-start | bytes 2621440 | tf_op jit(solution)/shard_map/all_gather | solution.py:71
  22.9 104.0 %all-gather.3.cloned.1.call-start = ((), (), s32[]{:S(2)}) async-start(), calls=%async_computation.6 | async-start | bytes 4096000 | tf_op jit(solution)/shard_map/all_gather | solution.py:50
  98.4 130.1 %reduce-scatter.8.cloned.1.call-start = ((), (), s32[]{:S(2)}) async-start(), calls=%async_computation.10 | async-start | bytes 8192000 | tf_op jit(solution)/shard_map/reduce_scatter | solution.py:88
  98.7 28.2 %copy-start.7 = (bf16[512,2048]{1,0:T(8,128)(2,1)S(1)}, bf16[512,2048]{1,0:T(8,128)(2,1)}, u32[]{:S(2)}) copy-start(bf16[512,2048]{1,0:T(8,128)(2,1)} %param.13) | copy-start | bytes 6291460
  126.9 11.7 %copy-start.4 = (f32[2048]{0:T(1024)S(1)}, f32[2048]{0:T(1024)}, u32[]{:S(2)}) copy-start(f32[2048]{0:T(1024)} %param.15) | copy-start | bytes 24580
  126.9 11.7 %copy-start.6 = (bf16[2048,1024]{1,0:T(8,128)(2,1)S(1)}, bf16[2048,1024]{1,0:T(8,128)(2,1)}, u32[]{:S(2)}) copy-start(bf16[2048,1024]{1,0:T(8,128)(2,1)} %param.17) | copy-start | bytes 12582916
  126.9 11.7 %copy-start.8 = (bf16[2,512,1024]{2,1,0:T(8,128)(2,1)S(1)}, bf16[2,512,1024]{2,1,0:T(8,128)(2,1)}, u32[]{:S(2)}) copy-start(bf16[2,512,1024]{2,1,0:T(8,128)(2,1)} %all-gather.5.cloned.1.call-done) | copy-start | bytes 6291460
  126.9 11.7 %copy-start.9 = (f32[512,2048]{1,0:T(8,128)S(1)}, f32[512,2048]{1,0:T(8,128)}, u32[]{:S(2)}) copy-start(f32[512,2048]{1,0:T(8,128)} %fusion.27) | copy-start | bytes 12582916
  138.5 4.7 %copy-start.1 = (bf16[2,256,2048]{2,1,0:T(8,128)(2,1)}, bf16[2,256,2048]{2,1,0:T(8,128)(2,1)S(1)}, u32[]{:S(2)}) copy-start(bf16[2,256,2048]{2,1,0:T(8,128)(2,1)S(1)} %get-tuple-element.12) | copy-start | bytes 6291460
  166.6 100.8 %reduce-scatter.4.cloned.1.call-start = ((), (), s32[]{:S(2)}) async-start(), calls=%async_computation.7 | async-start | bytes 2621440 | tf_op jit(solution)/shard_map/reduce_scatter | solution.py:65
  172.6 123.1 %reduce-scatter.6.cloned.1.call-start = ((), (), s32[]{:S(2)}) async-start(), calls=%async_computation.8 | async-start | bytes 2621440 | tf_op jit(solution)/shard_map/reduce_scatter | solution.py:66
  263.9 33.6 %all-to-all-start.2 = ((bf16[8,64,400]{2,1,0:T(8,128)(2,1)}), bf16[8,64,400]{2,1,0:T(8,128)(2,1)S(1)}, u32[]{:S(2)}, u32[]{:S(2)}) async-start(bf16[8,64,400]{2,1,0:T(8,128)(2,1)} %copy.27), calls=%async_computation.5 | async-start | bytes 1048576 | tf_op jit(solution)/shard_map/all_to_all | solution.py:100
  269.2 29.5 %copy-start = (bf16[64,3200]{1,0:T(8,128)(2,1)S(1)}, bf16[64,3200]{1,0:T(8,128)(2,1)}, u32[]{:S(2)}) copy-start(bf16[64,3200]{1,0:T(8,128)(2,1)} %param.10) | copy-start | bytes 1228804
  269.2 29.5 %copy-start.3 = (f32[3200]{0:T(1024)S(1)}, f32[3200]{0:T(1024)}, u32[]{:S(2)}) copy-start(f32[3200]{0:T(1024)} %param.11) | copy-start | bytes 38404
Sparse Core Ops, SparseCore 0:
  23.3 24.2 all-gather.4
  98.5 28.3 all-gather.2
  166.8 61.6 reduce-scatter.7
  230.9 31.1 reduce-scatter.3
  264.5 31.1 reduce-scatter.5
where the time goes:
time: 307 us
  waiting for transfers between devices  169 us (55%)
  matrix products  52.6 us (17%)
  blocking collectives  32.8 us (11%)
  other arithmetic  19.4 us (6%)
  between operations  14 us (5%)
  starting transfers between devices  11.1 us (4%)
  local copies, waits for them, and re-layouts  7.95 us (3%)
    all_to_all x1, waiting for transfers between devices, shards(): lax.all_to_all(outbox, 'dp', split_axis=0, concat_axis=0, tiled=True)  71.5 us
    reduce_scatter x1, waiting for transfers between devices, shards(): lax.psum_scatter(jnp.einsum('srd,vd->rsv', piece, w_proj, preferred_eleme...  49.2 us
    all_to_all x1, blocking collectives, shards(): lax.all_to_all(d_vis_slots[None], 'dp', split_axis=3, concat_axis=0, tile...  26.8 us
    reduce_scatter x1, waiting for transfers between devices, shards(): lax.psum_scatter(value_part, 'mp', scatter_dimension=1, tiled=True)  26.5 us
    all_gather x1, waiting for transfers between devices, shards(): lax.all_gather(arrived, 'mp', axis=1, tiled=True)  21.2 us
    dot_general x1, matrix products, shards(): jnp.einsum('srd,vd->rsv', piece, w_proj, preferred_element_type=jnp.float32)  12.6 us
    dot_general x1, matrix products, shards(): jnp.einsum('srv,vd->srd', lax.all_gather(arrived, 'mp', axis=1, tiled=Tru...  11.6 us
    all_to_all x1, starting transfers between devices, shards(): lax.all_to_all(outbox, 'dp', split_axis=0, concat_axis=0, tiled=True)  7.41 us
  transfers between devices with their start and end apart: 7, of which 4 were waited for; matrix products, arithmetic and copies ran while one was open for 12% of the time, Pallas kernels for 0%

commit v1 on v0

v1 whole, which is shorter than its diff:
```python
import jax
import jax.numpy as jnp
from jax import lax
from jax.sharding import PartitionSpec as P

PATCH = 256
F32 = jnp.float32
BF16 = jnp.bfloat16


def shards(vision, vision_gain, image_slot, text_embed, w_proj, llm_gain, w_key, w_value, key_grad, value_grad):
    mp = lax.axis_size("mp")
    here = lax.axis_index("dp")
    tokens_dev, width = text_embed.shape
    slot_dev = tokens_dev // PATCH
    d_model = width * mp
    kvd = key_grad.shape[1]
    vision_f = vision.astype(F32)
    vis_scale = lax.rsqrt(jnp.mean(vision_f * vision_f, axis=1, keepdims=True) + 1e-06)
    vis_normed = (vision_f * vis_scale * vision_gain).astype(BF16)
    vis_all = lax.all_gather(vis_normed, "mp", axis=0, tiled=True)
    grads = jnp.concatenate([key_grad, value_grad], axis=1)
    every = lax.all_gather(grads, "dp", axis=0, tiled=True)
    my_slot = lax.dynamic_index_in_dim(image_slot, here, keepdims=False)
    mine = lax.dynamic_slice_in_dim(every, my_slot * PATCH, PATCH, axis=0)
    both = jnp.concatenate([grads, mine], axis=0)
    stacked = lax.all_gather(both, "mp", axis=0)
    g_key = jnp.concatenate([stacked[m, :, :kvd] for m in range(mp)], axis=1)
    g_val = jnp.concatenate([stacked[m, :, kvd:] for m in range(mp)], axis=1)
    image_embed = jnp.dot(vis_all, w_proj, preferred_element_type=F32).astype(BF16)

    def forward(e):
        ef = e.astype(F32)
        x = (ef * llm_gain).astype(BF16)
        k = jnp.dot(x, w_key, preferred_element_type=F32)
        v = jnp.dot(x, w_value, preferred_element_type=F32)
        return jnp.sum(ef * ef, axis=1), k, v

    sq_t, k_t, v_t = forward(text_embed)
    sq_i, k_i, v_i = forward(image_embed)
    k_all = jnp.concatenate([k_t, k_i], axis=0)
    v_all = jnp.concatenate([v_t, v_i], axis=0)
    inner = jnp.sum(g_key.astype(F32) * k_all + g_val.astype(F32) * v_all, axis=1)
    sq = lax.psum(jnp.concatenate([sq_t, sq_i]), "mp")
    inner = lax.psum(inner, "mp")
    scale = lax.rsqrt(sq / d_model + 1e-05)[:, None]
    kv = jnp.concatenate(
        [a[:, m * kvd:(m + 1) * kvd].astype(BF16) for m in range(mp) for a in (k_all, v_all)], axis=1
    )
    kv_sum = lax.psum_scatter(kv, "mp", scatter_dimension=1, tiled=True)
    kv_out = (kv_sum.astype(F32) * scale).astype(BF16)
    kv_text, kv_img = kv_out[:tokens_dev], kv_out[tokens_dev:]
    kv_every = lax.all_gather(kv_img, "dp", axis=0)
    blocks = []
    fills = []
    for s in range(slot_dev):
        hit = image_slot == here * slot_dev + s
        filled = jnp.any(hit)
        owner = jnp.argmax(hit)
        got = lax.dynamic_index_in_dim(kv_every, owner, keepdims=False)
        blocks.append(jnp.where(filled, got, kv_text[s * PATCH:(s + 1) * PATCH]))
        fills.append(filled)
    kv_final = jnp.concatenate(blocks, axis=0)
    contract = (((1,), (1,)), ((), ()))
    coef = scale * scale * scale * (inner / d_model)[:, None]

    def backward(gk, gv, e, sc, co):
        d = lax.dot_general(gk, w_key, contract, preferred_element_type=F32)
        d = d + lax.dot_general(gv, w_value, contract, preferred_element_type=F32)
        return sc * (d * llm_gain) - e.astype(F32) * co

    t = tokens_dev
    d_image = backward(g_key[t:], g_val[t:], image_embed, scale[t:], coef[t:]).astype(BF16)
    d_rows = lax.dot_general(d_image, w_proj, contract, preferred_element_type=F32).astype(BF16)
    d_vis = lax.psum_scatter(d_rows, "mp", scatter_dimension=0, tiled=True).astype(F32)
    d_text = backward(g_key[:t], g_val[:t], text_embed, scale[:t], coef[:t])
    full = jnp.repeat(jnp.stack(fills), PATCH)[:, None]
    text_grad = jnp.where(full, 0.0, d_text).astype(BF16)
    grad_h = d_vis * vision_gain
    vis_inner = jnp.mean(grad_h * vision_f, axis=1, keepdims=True)
    vision_grad = vis_scale * grad_h - vision_f * vis_scale * vis_scale * vis_scale * vis_inner
    return kv_final[:, :kvd], kv_final[:, kvd:], text_grad, vision_grad.astype(BF16)


def solution(mesh):
    placed = (
        P(("dp", "mp"), None),
        P(),
        P(),
        P("dp", "mp"),
        P(None, "mp"),
        P("mp"),
        P("mp", None),
        P("mp", None),
        P("dp", "mp"),
        P("dp", "mp"),
    )
    return jax.shard_map(
        shards,
        mesh=mesh,
        in_specs=placed,
        out_specs=(P("dp", "mp"), P("dp", "mp"), P("dp", "mp"), P(("dp", "mp"), None)),
        check_vma=False,
    )
```

time: 307 us -> 270 us (0.88)
  blocking collectives: 32.8 us -> 6.13 us
  waiting for transfers between devices: 169 us -> 154 us
  starting transfers between devices: 11.1 us -> 0.43 us
  local copies, waits for them, and re-layouts: 7.95 us -> 18.5 us
  between operations: 14 us -> 19.1 us
  matrix products: 52.6 us -> 48.7 us
  other arithmetic: 19.4 us -> 23.1 us
    all_gather x2 -> x4, waiting for transfers between devices: 21.3 us -> 133 us  [the longest x1 66.5 us: shards(): every = lax.all_gather(grads, 'dp', axis=0, tiled=True)]
    all_to_all x2 -> x0, waiting for transfers between devices: 71.6 us -> none  [the longest x1 71.5 us: shards(): lax.all_to_all(outbox, 'dp', split_axis=0, concat_axis=0, tiled=True)]
    reduce_scatter x3 -> x2, waiting for transfers between devices: 75.7 us -> 20.7 us  [the longest x1 12 us: shards(): lax.psum_scatter(d_rows, 'mp', scatter_dimension=0, tiled=True).astype(F32)]
    all_to_all x1 -> x0, blocking collectives: 26.8 us -> none  [shards(): lax.all_to_all(d_vis_slots[None], 'dp', split_axis=3, concat_axis=0, tile...]
    all_to_all x2 -> x0, starting transfers between devices: 10.9 us -> none  [the longest x1 7.41 us: shards(): lax.all_to_all(outbox, 'dp', split_axis=0, concat_axis=0, tiled=True)]
    unnamed x23 -> x66, local copies, waits for them, and re-layouts: 2.03 us -> 12.1 us
    convert_element_type x6 -> x3, other arithmetic: 10.5 us -> 5.34 us  [the longest x1 2.06 us: shards(): vision_grad.astype(BF16)]
    concatenate x0 -> x5, other arithmetic: none -> 4.95 us  [the longest x1 1.74 us: shards(): g_key = jnp.concatenate([stacked[m, :, :kvd] for m in range(mp)], axis=1)]
  transfers between devices with their start and end apart: 7 -> 6, of which waited for: 4 -> 6; matrix products, arithmetic and copies ran while one was open for 12% -> 30% of each run, Pallas kernels for 0% -> 0%
where the time goes in v1:
time: 270 us
  waiting for transfers between devices  154 us (57%)
  matrix products  48.7 us (18%)
  other arithmetic  23.1 us (9%)
  between operations  19.1 us (7%)
  local copies, waits for them, and re-layouts  18.5 us (7%)
  blocking collectives  6.13 us (2%)
    all_gather x1, waiting for transfers between devices, shards(): every = lax.all_gather(grads, 'dp', axis=0, tiled=True)  66.5 us
    all_gather x1, waiting for transfers between devices, shards(): kv_every = lax.all_gather(kv_img, 'dp', axis=0)  48.4 us
    dot_general x1, matrix products, shards(): lax.dot_general(d_image, w_proj, contract, preferred_element_type=F32)  13.3 us
    all_gather x1, waiting for transfers between devices, shards(): vis_all = lax.all_gather(vis_normed, 'mp', axis=0, tiled=True)  12.2 us
    unnamed x66, local copies, waits for them, and re-layouts  12.1 us
    reduce_scatter x1, waiting for transfers between devices, shards(): lax.psum_scatter(d_rows, 'mp', scatter_dimension=0, tiled=True).astype(F32)  12 us
    dot_general x1, matrix products, shards(): jnp.dot(vis_all, w_proj, preferred_element_type=F32).astype(BF16)  9.13 us
    reduce_scatter x1, waiting for transfers between devices, shards(): kv_sum = lax.psum_scatter(kv, 'mp', scatter_dimension=1, tiled=True)  8.65 us
  transfers between devices with their start and end apart: 6, of which 6 were waited for; matrix products, arithmetic and copies ran while one was open for 30% of the time, Pallas kernels for 0%

profile of v1, /device:TPU:0, one launch (start us, length us, event | category | flops | bytes accessed | tf_op | source)
XLA Modules:
  0.0 269.7 jit_solution(11849882962777633755)
XLA Ops:
  11.2 1.9 fusion.26
  14.5 5.2 %fusion.13 = f32[512,1024]{1,0:T(8,128)S(1)} fusion(bf16[2048,1024]{1,0:T(8,128)(2,1)} %param.17, bf16[512,2048]{1,0:T(8,128)(2,1)} %param.13, f32[2048]{0:T(1024)S(1)} %copy-done.25), kind=kOutput, calls=%fused_computation.25 | convolution fusion | flops 2150629376 | bytes 8396800 | tf_op jit(solution)/shard_map/dot_general | solution.py:36
  19.7 66.5 %all-gather.9.cloned.1.call-done = bf16[4096,512]{1,0:T(8,128)(2,1)} async-done(((bf16[512,512]{1,0:T(8,128)(2,1)}), bf16[4096,512]{1,0:T(8,128)(2,1)}) %all-gather.9.cloned.1.call-update) | async-done | bytes 4194320 | tf_op jit(solution)/shard_map/all_gather | solution.py:23
  88.3 6.5 %fusion.15 = f32[512,1024]{1,0:T(8,128)} fusion(bf16[2048,1024]{1,0:T(8,128)(2,1)} %param.16, bf16[512,2048]{1,0:T(8,128)(2,1)} %param.13, f32[2048]{0:T(1024)S(1)} %copy-done.25), kind=kOutput, calls=%fused_computation.26 | convolution fusion | flops 2150629376 | bytes 8396800 | tf_op jit(solution)/shard_map/dot_general | solution.py:35
  94.7 12.2 %all-gather.7.cloned.1.call-done = bf16[256,3200]{1,0:T(8,128)(2,1)} async-done(((bf16[64,3200]{1,0:T(8,128)(2,1)}), bf16[256,3200]{1,0:T(8,128)(2,1)}) %all-gather.7.cloned.1.call-update) | async-done | bytes 1638416 | tf_op jit(solution)/shard_map/all_gather | solution.py:21
  106.9 9.1 %fusion.12 = (f32[256]{0:T(256)S(1)}, bf16[256,2048]{1,0:T(8,128)(2,1)S(1)}) fusion(bf16[256,3200]{1,0:T(8,128)(2,1)} %all-gather.7.cloned.1.call-done, bf16[3200,2048]{1,0:T(8,128)(2,1)} %param.14), kind=kOutput, calls=%fused_computation.24 | convolution fusion | flops 3357540096 | bytes 15795200 | tf_op jit(solution)/shard_map/dot_general | solution.py:30
  118.6 1.9 copy-done.23
  129.0 2.1 fusion.1
  131.1 5.9 %all-gather.13.cloned.1.call-done = bf16[3072,512]{1,0:T(8,128)(2,1)} async-done(((bf16[768,512]{1,0:T(8,128)(2,1)}), bf16[3072,512]{1,0:T(8,128)(2,1)}) %all-gather.13.cloned.1.call-update) | async-done | bytes 3145744 | tf_op jit(solution)/shard_map/all_gather | solution.py:27
  137.1 2.2 slice_bitcast_fusion.7
  140.8 2.4 add_reduce_fusion
  143.2 6.1 %all-reduce = (f32[768]{0:T(1024)S(1)}, f32[768]{0:T(1024)S(1)}) all-reduce(f32[768]{0:T(1024)S(1)} %pad_maximum_fusion.6, f32[768]{0:T(1024)S(1)} %add_reduce_fusion), channel_id=1, replica_groups=mesh['dp'=8,'mp'=4] {'mp'}, use_global_device_ids=true, to_apply=%region_5.6 | all-reduce | flops 1536 | bytes 12288 | tf_op jit(solution)/shard_map/psum | solution.py:44
  149.4 1.7 pad_maximum_fusion.2
  151.1 1.4 pad_maximum_fusion.3
  152.6 2.6 fusion.35
  155.2 13.3 %convolution_convert_fusion = bf16[256,3200]{1,0:T(8,128)(2,1)} fusion(bf16[3200,2048]{1,0:T(8,128)(2,1)} %param.14, f32[256,2048]{1,0:T(8,128)} %fusion.35, bf16[2048,1024]{1,0:T(8,128)(2,1)} %param.17, bf16[256,2048]{1,0:T(8,128)(2,1)S(1)} %copy-done.28, f32[256]{0:T(256)S(1)} %slice.130, f32[256]{0:T(256)S(1)} %slice.127, f32[2048]{0:T(1024)S(1)} %copy-done.26, ...), kind=kOutput, calls=%fused_computation.3 | convolution fusion | flops 4433674240 | bytes 22620160 | tf_op jit(solution)/shard_map/dot_general | solution.py:74
  168.5 8.7 %reduce-scatter.3.cloned.1.call-done = bf16[768,512]{1,0:T(8,128)(2,1)} async-done(((bf16[768,2048]{1,0:T(8,128)(2,1)}), bf16[768,512]{1,0:T(8,128)(2,1)}) %reduce-scatter.3.cloned.1.call-update) | async-done | bytes 786448 | tf_op jit(solution)/shard_map/reduce_scatter | solution.py:50
  177.2 1.4 multiply_convert_fusion
  186.6 4.9 %fusion.18 = f32[512,2048]{1,0:T(8,128)S(1)} fusion(bf16[2048,1024]{1,0:T(8,128)(2,1)} %param.16, bf16[768,1024]{1,0:T(8,128)(2,1)S(1)} %pad_maximum_fusion.2), kind=kOutput, calls=%fused_computation.34 | convolution fusion | flops 2147483648 | bytes 9437184 | tf_op jit(solution)/shard_map/dot_general | solution.py:68
  191.6 4.5 %fusion.4 = bf16[512,2048]{1,0:T(8,128)(2,1)} fusion(bf16[512,2048]{1,0:T(8,128)(2,1)S(1)} %copy-done.17, f32[512,2048]{1,0:T(8,128)S(1)} %fusion.18, bf16[2048,1024]{1,0:T(8,128)(2,1)S(1)} %copy-done.24, f32[512]{0:T(512)S(1)} %slice.126, f32[512]{0:T(512)S(1)} %slice.115, f32[2048]{0:T(1024)S(1)} %copy-done.26, pred[512]{0:T(512)(128)(4,1)S(1)} %broadcast_in_dim.17, ...), kind=kOutput, calls=%fused_computation.8 | convolution fusion | flops 2155872256 | bytes 13644288 | tf_op jit(solution)/shard_map/dot_general | solution.py:69
  196.1 12.0 %reduce-scatter.5.cloned.1.call-done = bf16[64,3200]{1,0:T(8,128)(2,1)} async-done(((bf16[256,3200]{1,0:T(8,128)(2,1)}), bf16[64,3200]{1,0:T(8,128)(2,1)}) %reduce-scatter.5.cloned.1.call-update) | async-done | bytes 409616 | tf_op jit(solution)/shard_map/reduce_scatter | solution.py:75
  209.4 2.1 fusion.30
  211.4 48.4 %all-gather.11.cloned.1.call-done = bf16[2048,512]{1,0:T(8,128)(2,1)} async-done(((bf16[256,512]{1,0:T(8,128)(2,1)}), bf16[2048,512]{1,0:T(8,128)(2,1)}) %all-gather.11.cloned.1.call-update) | async-done | bytes 2097168 | tf_op jit(solution)/shard_map/all_gather | solution.py:53
  259.8 2.3 slice_select_fusion
  (104 shorter events, 25.3 us)
Async XLA Ops:
  7.2 6.1 %copy-start.20 = (s32[8]{0:T(128)S(1)}, s32[8]{0:T(128)}, u32[]{:S(2)}) copy-start(s32[8]{0:T(128)} %param.12) | copy-start | bytes 100
  7.2 7.3 %copy-start.25 = (f32[2048]{0:T(1024)S(1)}, f32[2048]{0:T(1024)}, u32[]{:S(2)}) copy-start(f32[2048]{0:T(1024)} %param.15) | copy-start | bytes 24580
  7.2 79.1 %all-gather.9.cloned.1.call-start = ((), (), s32[]{:S(2)}) async-start(), calls=%async_computation.4 | async-start | bytes 4718592 | tf_op jit(solution)/shard_map/all_gather | solution.py:23
  10.0 96.9 %all-gather.7.cloned.1.call-start = ((), (), s32[]{:S(2)}) async-start(), calls=%async_computation.2 | async-start | bytes 2048000 | tf_op jit(solution)/shard_map/all_gather | solution.py:21
  13.2 123.9 %all-gather.13.cloned.1.call-start = ((), (), s32[]{:S(2)}) async-start(), calls=%async_computation.7 | async-start | bytes 3932160 | tf_op jit(solution)/shard_map/all_gather | solution.py:27
  14.5 72.7 %copy-start.16 = (bf16[512,512]{1,0:T(8,128)(2,1)S(1)}, bf16[512,512]{1,0:T(8,128)(2,1)}, u32[]{:S(2)}) copy-start(bf16[512,512]{1,0:T(8,128)(2,1)} %copy-done.15) | copy-start | bytes 1572868
  88.2 89.0 %reduce-scatter.3.cloned.1.call-start = ((), (), s32[]{:S(2)}) async-start(), calls=%async_computation.3 | async-start | bytes 3932160 | tf_op jit(solution)/shard_map/reduce_scatter | solution.py:50
  106.9 9.1 %copy-start.21 = (bf16[2048,1024]{1,0:T(8,128)(2,1)S(1)}, bf16[2048,1024]{1,0:T(8,128)(2,1)}, u32[]{:S(2)}) copy-start(bf16[2048,1024]{1,0:T(8,128)(2,1)} %param.16) | copy-start | bytes 12582916
  116.1 2.5 copy-start.27
  128.8 79.3 %reduce-scatter.5.cloned.1.call-start = ((), (), s32[]{:S(2)}) async-start(), calls=%async_computation.5 | async-start | bytes 2048000 | tf_op jit(solution)/shard_map/reduce_scatter | solution.py:75
  137.1 3.7 %copy-start.1 = (f32[512,1024]{1,0:T(8,128)S(1)}, f32[512,1024]{1,0:T(8,128)}, u32[]{:S(2)}) copy-start(f32[512,1024]{1,0:T(8,128)} %fusion.15) | copy-start | bytes 6291460
  137.1 3.7 %copy-start.4 = (f32[256,1024]{1,0:T(8,128)S(1)}, f32[256,1024]{1,0:T(8,128)}, u32[]{:S(2)}) copy-start(f32[256,1024]{1,0:T(8,128)} %copy-done.3) | copy-start | bytes 3145732
  143.1 8.0 %copy-start.6 = (bf16[768,256]{1,0:T(8,128)(2,1)S(1)}, bf16[768,256]{1,0:T(8,128)(2,1)}, u32[]{:S(2)}) copy-start(bf16[768,256]{1,0:T(8,128)(2,1)} %copy-done.5) | copy-start | bytes 1179652
  143.1 8.0 %copy-start.8 = (bf16[768,256]{1,0:T(8,128)(2,1)S(1)}, bf16[768,256]{1,0:T(8,128)(2,1)}, u32[]{:S(2)}) copy-start(bf16[768,256]{1,0:T(8,128)(2,1)} %copy-done.7) | copy-start | bytes 1179652
  143.2 8.0 %copy-start.10 = (bf16[768,256]{1,0:T(8,128)(2,1)S(1)}, bf16[768,256]{1,0:T(8,128)(2,1)}, u32[]{:S(2)}) copy-start(bf16[768,256]{1,0:T(8,128)(2,1)} %copy-done.9) | copy-start | bytes 1179652
  149.3 3.2 %copy-start.22 = (bf16[2048,1024]{1,0:T(8,128)(2,1)S(1)}, bf16[2048,1024]{1,0:T(8,128)(2,1)}, u32[]{:S(2)}) copy-start(bf16[2048,1024]{1,0:T(8,128)(2,1)} %param.16) | copy-start | bytes 12582916
  152.6 2.6 copy-start.26
  152.6 2.6 copy-start.28
  168.5 91.3 %all-gather.11.cloned.1.call-start = ((), (), s32[]{:S(2)}) async-start(), calls=%async_computation.6 | async-start | bytes 2359296 | tf_op jit(solution)/shard_map/all_gather | solution.py:53
  186.5 5.0 %copy-start.17 = (bf16[512,2048]{1,0:T(8,128)(2,1)S(1)}, bf16[512,2048]{1,0:T(8,128)(2,1)}, u32[]{:S(2)}) copy-start(bf16[512,2048]{1,0:T(8,128)(2,1)} %param.13) | copy-start | bytes 6291460
  186.6 5.0 %copy-start.18 = (bf16[768,1024]{1,0:T(8,128)(2,1)S(1)}, bf16[768,1024]{1,0:T(8,128)(2,1)}, u32[]{:S(2)}) copy-start(bf16[768,1024]{1,0:T(8,128)(2,1)} %pad_maximum_fusion.3) | copy-start | bytes 4718596
  186.6 5.0 %copy-start.24 = (bf16[2048,1024]{1,0:T(8,128)(2,1)S(1)}, bf16[2048,1024]{1,0:T(8,128)(2,1)}, u32[]{:S(2)}) copy-start(bf16[2048,1024]{1,0:T(8,128)(2,1)} %param.17) | copy-start | bytes 12582916
  191.6 16.5 %copy-start.2 = (bf16[64,3200]{1,0:T(8,128)(2,1)S(1)}, bf16[64,3200]{1,0:T(8,128)(2,1)}, u32[]{:S(2)}) copy-start(bf16[64,3200]{1,0:T(8,128)(2,1)} %param.10) | copy-start | bytes 1228804
  191.6 16.5 %copy-start.19 = (f32[3200]{0:T(1024)S(1)}, f32[3200]{0:T(1024)}, u32[]{:S(2)}) copy-start(f32[3200]{0:T(1024)} %param.11) | copy-start | bytes 38404
  (11 other events, 15.1 us)
Sparse Core Ops, SparseCore 0:
  10.7 75.5 all-gather.8
  88.4 18.5 all-gather.6
  108.5 28.4 all-gather.12
  139.4 37.7 reduce-scatter.2
  179.6 28.4 reduce-scatter.4
  210.7 49.0 all-gather.10

commit v2 on v1

v2 whole, which is shorter than its diff:
```python
import functools

import jax
import jax.numpy as jnp
from jax import lax
from jax.experimental import pallas as pl
from jax.experimental.pallas import tpu as pltpu
from jax.sharding import PartitionSpec as P

PATCH = 256
F32 = jnp.float32
BF16 = jnp.bfloat16
NT = (((1,), (1,)), ((), ()))
DMA = pltpu.SemaphoreType.DMA


def nt(a, b):
    return lax.dot_general(a, b, NT, preferred_element_type=F32)


def remote(src, dst, send_sem, recv_sem, device):
    return pltpu.make_async_remote_copy(
        src_ref=src, dst_ref=dst, send_sem=send_sem, recv_sem=recv_sem,
        device_id=device, device_id_type=pl.DeviceIdType.MESH,
    )


def to_rows(sq, inner):
    lane = lax.broadcasted_iota(jnp.int32, (sq.shape[0], 128), 1)
    wide = jnp.where(lane == 0, sq, jnp.where(lane == 1, inner, 0.0))
    return jnp.transpose(wide)[:8]


def to_columns(rows):
    wide = jnp.transpose(jnp.concatenate([rows] * 16, axis=0))
    return wide[:, 0:1], wide[:, 1:2]


def kernel(
    dp, mp, slot_ref, owner_ref, vision_h, vgain, text_h, wp_h, gain, wk_h, wv_h, kg_h, vg_h, kg4, vg4,
    kvt_out, kvs_out, tg_h, vg_out,
    vis, vis_all, text, wp, wk, wv, xt, gk, gv, gik, giv, emb, xi, dimg, dg,
    t_send, t_own, t_l1, t_s2, t_l2, i_send, i_own, i_l1, i_s2, i_l2,
    d_send, d_own, d_l1, d_s2, d_l2, kvt, kvi,
    st_t, sr_t, st_i, sr_i, sc_t, co_t, sc_i, co_i,
    r1k, r1v, s2k, s2v, r2k, r2v, kvb, r3, s4, r4, tg,
    load_sem, ag_s, ag_r, rs_s, rs_r, st_s, st_r, dv_s, dv_r,
    a1_s, a1_r, a2_s, a2_r, b1_s, b1_r, b2_s, b2_r, tg_sem,
):
    me_d = lax.axis_index("dp")
    me = lax.axis_index("mp")
    ycount = mp // 2
    core = lax.rem(me, 2)
    y = lax.div(me, 2)
    partner = y * 2 + (1 - core)
    tokens, width = text.shape
    slots = tokens // PATCH
    kvd = gk.shape[1] // mp
    rows = vis.shape[0]
    dv = vis.shape[1]
    d_model = width * mp
    rb = r1k.shape[1]

    def ynext(k):
        return lax.rem(y + k, ycount)

    def yprev(k):
        return lax.rem(y + ycount - k, ycount)

    def dnext(k):
        return lax.rem(me_d + k, dp)

    def dprev(k):
        return lax.rem(me_d + dp - k, dp)

    def col(m):
        return pl.ds(pl.multiple_of(m * kvd, kvd), kvd)

    sends = []

    def send(*args):
        copy = remote(*args)
        copy.start()
        sends.append(copy)

    loads = [
        (vision_h, vis), (kg_h, gk.at[:, col(me)]), (vg_h, gv.at[:, col(me)]),
        (text_h, text), (wk_h, wk), (wv_h, wv), (wp_h, wp),
        (kg4.at[:, me_d], r1k.at[pl.ds(me_d * slots, slots)]),
        (vg4.at[:, me_d], r1v.at[pl.ds(me_d * slots, slots)]),
    ]
    loads = [pltpu.make_async_copy(a, b, load_sem.at[n]) for n, (a, b) in enumerate(loads)]
    for copy in loads:
        copy.start()

    barrier = pltpu.get_barrier_semaphore()

    @pl.loop(1, dp)
    def _(k):
        pl.semaphore_signal(barrier, inc=1, device_id=(dnext(k), me), device_id_type=pl.DeviceIdType.MESH)

    for k in range(1, mp):
        pl.semaphore_signal(
            barrier, inc=1, device_id=(me_d, lax.rem(me + k, mp)), device_id_type=pl.DeviceIdType.MESH
        )

    loads[0].wait()
    vf = vis[...].astype(F32)
    vscale = lax.rsqrt(jnp.mean(vf * vf, axis=1, keepdims=True) + 1e-06)
    vis_all[me] = (vf * vscale * vgain[...]).astype(BF16)
    pl.semaphore_wait(barrier, dp - 1 + mp - 1)

    def gather_start(g, block):
        for k in range(1, ycount):
            send(block(me), block(me), ag_s.at[g, 0, k], ag_r.at[g, 0, k], (me_d, ynext(k) * 2 + core))
        send(block(me), block(me), ag_s.at[g, 0, 0], ag_r.at[g, 0, 0], (me_d, partner))

    def arrived(block, send_sem, recv_sem):
        remote(block, block, send_sem, recv_sem, (me_d, partner)).wait_recv()

    def gather_relay(g, block):
        for k in range(1, ycount):
            got = block(yprev(k) * 2 + core)
            arrived(got, ag_s.at[g, 0, k], ag_r.at[g, 0, k])
            send(got, got, ag_s.at[g, 1, k], ag_r.at[g, 1, k], (me_d, partner))

    def gather_finish(g, block):
        arrived(block(partner), ag_s.at[g, 0, 0], ag_r.at[g, 0, 0])
        for k in range(1, ycount):
            arrived(block(yprev(k) * 2 + 1 - core), ag_s.at[g, 1, k], ag_r.at[g, 1, k])

    vis_block = lambda m: vis_all.at[m]
    gk_block = lambda m: gk.at[:, col(m)]
    gv_block = lambda m: gv.at[:, col(m)]
    gik_block = lambda m: gik.at[:, col(m)]
    giv_block = lambda m: giv.at[:, col(m)]

    gather_start(0, vis_block)

    mine = pl.ds(me_d * slots, slots)

    def a1(k, which):
        src, dst = ((kg4, r1k), (vg4, r1v))[which]
        return remote(
            src.at[:, dnext(k)], dst.at[mine], a1_s.at[which, k], a1_r.at[which, k], (dnext(k), me)
        )

    @pl.loop(1, dp)
    def _(k):
        a1(k, 0).start()
        a1(k, 1).start()

    loads[1].wait()
    loads[2].wait()
    gather_start(1, gk_block)
    gather_start(2, gv_block)

    def stage(x, n, psend, own, l1):
        def chunk(m):
            k_part = jnp.dot(x[...], wk[:, col(m)], preferred_element_type=F32)
            v_part = jnp.dot(x[...], wv[:, col(m)], preferred_element_type=F32)
            return k_part, v_part

        for k in range(ycount):
            yk = ynext(k)
            k_part, v_part = chunk(yk * 2 + 1 - core)
            psend[yk, :, :kvd] = k_part.astype(BF16)
            psend[yk, :, kvd:] = v_part.astype(BF16)
            send(psend.at[yk], l1.at[yk], rs_s.at[n, 0, k], rs_r.at[n, 0, k], (me_d, partner))
        for k in range(ycount):
            yk = ynext(k)
            k_part, v_part = chunk(yk * 2 + core)
            own[yk, :, :kvd] = k_part
            own[yk, :, kvd:] = v_part

    def level_two(n, own, l1, s2, l2):
        for k in range(ycount - 1, 0, -1):
            yk = ynext(k)
            arrived(l1.at[yk], rs_s.at[n, 0, k], rs_r.at[n, 0, k])
            s2[k] = (own[yk] + l1[yk].astype(F32)).astype(BF16)
            send(s2.at[k], l2.at[k], rs_s.at[n, 1, k], rs_r.at[n, 1, k], (me_d, yk * 2 + core))

    def level_end(n, own, l1, l2):
        arrived(l1.at[y], rs_s.at[n, 0, 0], rs_r.at[n, 0, 0])
        total = own[y] + l1[y].astype(F32)
        for k in range(1, ycount):
            arrived(l2.at[k], rs_s.at[n, 1, k], rs_r.at[n, 1, k])
            total = total + l2[k].astype(F32)
        return total

    def stats_send(n, st, sr):
        for k in range(1, mp):
            send(st, sr.at[k], st_s.at[n, k], st_r.at[n, k], (me_d, lax.rem(me + k, mp)))

    def stats_end(n, st, sr, sc, co):
        total = st[...]
        for k in range(1, mp):
            arrived(sr.at[k], st_s.at[n, k], st_r.at[n, k])
            total = total + sr[k]
        sq, inner = to_columns(total)
        scale = lax.rsqrt(sq / d_model + 1e-05)
        sc[...] = jnp.broadcast_to(scale, sc.shape)
        co[...] = jnp.broadcast_to(scale * scale * scale * (inner / d_model), co.shape)

    loads[3].wait()
    tf = text[...].astype(F32)
    sq_t = jnp.sum(tf * tf, axis=1, keepdims=True)
    xt[...] = (tf * gain[...]).astype(BF16)
    loads[4].wait()
    loads[5].wait()
    stage(xt, 0, t_send, t_own, t_l1)
    gather_relay(0, vis_block)
    level_two(0, t_own, t_l1, t_s2, t_l2)

    loads[7].wait()
    loads[8].wait()

    @pl.loop(1, dp)
    def _(k):
        for which, dst in ((0, r1k), (1, r1v)):
            block = dst.at[pl.ds(dprev(k) * slots, slots)]
            remote(block, block, a1_s.at[which, k], a1_r.at[which, k], (me_d, partner)).wait_recv()

    @pl.loop(0, dp)
    def _(i):
        s2k[i] = r1k[slot_ref[i]]
        s2v[i] = r1v[slot_ref[i]]

    r2k[me_d] = s2k[me_d]
    r2v[me_d] = s2v[me_d]

    def a2(k, which):
        src, dst = ((s2k, r2k), (s2v, r2v))[which]
        return remote(
            src.at[dnext(k)], dst.at[me_d], a2_s.at[which, k], a2_r.at[which, k], (dnext(k), me)
        )

    @pl.loop(1, dp)
    def _(k):
        a2(k, 0).start()
        a2(k, 1).start()

    gather_finish(0, vis_block)
    loads[6].wait()
    step = 256
    dimg_rows = mp * rows


    def project(j, acc):
        cs = pl.ds(pl.multiple_of(j * step, step), step)
        e = jnp.concatenate([vis_all[m] for m in range(mp)], axis=0)
        e = jnp.dot(e, wp[:, cs], preferred_element_type=F32).astype(BF16)
        emb[:, cs] = e
        ef = e.astype(F32)
        xi[:, cs] = (ef * gain[:, cs]).astype(BF16)
        return acc + jnp.sum(ef * ef, axis=1, keepdims=True)

    sq_i = lax.fori_loop(0, width // step, project, jnp.zeros((dimg_rows, 1), F32))
    stage(xi, 1, i_send, i_own, i_l1)
    gather_relay(1, gk_block)
    gather_relay(2, gv_block)
    level_two(1, i_own, i_l1, i_s2, i_l2)

    @pl.loop(1, dp)
    def _(k):
        for which, dst in ((0, r2k), (1, r2v)):
            block = dst.at[dprev(k)]
            remote(block, block, a2_s.at[which, k], a2_r.at[which, k], (me_d, partner)).wait_recv()

    own_k = r2k[...].astype(F32).reshape(PATCH, kvd)
    own_v = r2v[...].astype(F32).reshape(PATCH, kvd)
    gik[:, col(me)] = own_k.astype(BF16)
    giv[:, col(me)] = own_v.astype(BF16)
    gather_start(3, gik_block)
    gather_start(4, giv_block)

    total = level_end(0, t_own, t_l1, t_l2)
    kvt[...] = total
    inner = jnp.sum(
        total[:, :kvd] * gk[:, col(me)].astype(F32) + total[:, kvd:] * gv[:, col(me)].astype(F32),
        axis=1, keepdims=True,
    )
    st_t[...] = to_rows(sq_t, inner)
    stats_send(0, st_t, sr_t)
    gather_finish(1, gk_block)
    gather_finish(2, gv_block)
    stats_end(0, st_t, sr_t, sc_t, co_t)
    kvt_out[...] = (kvt[...] * sc_t[:, 0:1]).astype(BF16)

    def text_copy(j):
        cs = pl.ds(pl.multiple_of(j * step, step), step)
        return pltpu.make_async_copy(tg.at[:, cs], tg_h.at[:, cs], tg_sem.at[j])

    def text_back(j, _):
        cs = pl.ds(pl.multiple_of(j * step, step), step)
        d = nt(gk[...], wk[cs, :]) + nt(gv[...], wv[cs, :])
        d = sc_t[:, 0:1] * (d * gain[:, cs]) - text[:, cs].astype(F32) * co_t[:, 0:1]
        tg[:, cs] = d.astype(BF16)
        text_copy(j).start()
        return 0

    lax.fori_loop(0, width // step, text_back, 0)

    total = level_end(1, i_own, i_l1, i_l2)
    kvi[...] = total
    inner = jnp.sum(
        total[:, :kvd] * gik[:, col(me)].astype(F32) + total[:, kvd:] * giv[:, col(me)].astype(F32),
        axis=1, keepdims=True,
    )
    st_i[...] = to_rows(sq_i, inner)
    stats_send(1, st_i, sr_i)
    gather_relay(3, gik_block)
    gather_relay(4, giv_block)
    gather_finish(3, gik_block)
    gather_finish(4, giv_block)

    def image_back(j, _):
        cs = pl.ds(pl.multiple_of(j * step, step), step)
        dg[:, cs] = (nt(gik[...], wk[cs, :]) + nt(giv[...], wv[cs, :])) * gain[:, cs]
        return 0

    lax.fori_loop(0, width // step, image_back, 0)
    stats_end(1, st_i, sr_i, sc_i, co_i)
    kvb[...] = (kvi[...] * sc_i[:, 0:1]).reshape(dp, rb, 2 * kvd).astype(BF16)
    r3[me_d] = kvb[me_d]

    def b1(k):
        return remote(kvb.at[dnext(k)], r3.at[me_d], b1_s.at[k], b1_r.at[k], (dnext(k), me))

    @pl.loop(1, dp)
    def _(k):
        b1(k).start()

    def image_end(j, _):
        cs = pl.ds(pl.multiple_of(j * step, step), step)
        d = sc_i[:, 0:1] * dg[:, cs] - emb[:, cs].astype(F32) * co_i[:, 0:1]
        dimg[:, cs] = d.astype(BF16)
        return 0

    lax.fori_loop(0, width // step, image_end, 0)

    pieces = d_send.shape[0]
    span = dv // pieces

    def vis_chunk(j):
        d = nt(dimg[...], wp[j * span:(j + 1) * span, :]).reshape(ycount, 2, rows, span)
        for yi in range(ycount):
            a, b = d[yi, 0], d[yi, 1]
            first = core == 0
            d_own[j, yi] = jnp.where(first, a, b)
            d_send[j, yi] = jnp.where(first, b, a).astype(BF16)
        send(d_send.at[j], d_l1.at[j], dv_s.at[0, j, 0], dv_r.at[0, j, 0], (me_d, partner))

    def vis_two(j):
        arrived(d_l1.at[j], dv_s.at[0, j, 0], dv_r.at[0, j, 0])
        for k in range(1, ycount):
            yk = ynext(k)
            d_s2[j, k] = (d_own[j, yk] + d_l1[j, yk].astype(F32)).astype(BF16)
            send(d_s2.at[j, k], d_l2.at[j, k], dv_s.at[1, j, k], dv_r.at[1, j, k], (me_d, yk * 2 + core))

    def b2(k):
        return remote(s4.at[dnext(k)], r4.at[:, me_d], b2_s.at[k], b2_r.at[k], (dnext(k), me))

    for j in range(pieces):
        vis_chunk(j)
        if j > 0:
            vis_two(j - 1)
        if j == min(2, pieces - 1):

            @pl.loop(1, dp)
            def _(k):
                block = r3.at[dprev(k)]
                remote(block, block, b1_s.at[k], b1_r.at[k], (me_d, partner)).wait_recv()

            @pl.loop(0, dp)
            def _(d):
                for s in range(slots):
                    s4[d, s] = r3[owner_ref[d * slots + s]]

            for s in range(slots):
                r4[s, me_d] = s4[me_d, s]

            @pl.loop(1, dp)
            def _(k):
                b2(k).start()

    vis_two(pieces - 1)
    hs = []
    for j in range(pieces):
        d = d_own[j, y] + d_l1[j, y].astype(F32)
        for k in range(1, ycount):
            arrived(d_l2.at[j, k], dv_s.at[1, j, k], dv_r.at[1, j, k])
            d = d + d_l2[j, k].astype(F32)
        hs.append(d.astype(BF16).astype(F32))
    vf = vis[...].astype(F32)
    vscale = lax.rsqrt(jnp.mean(vf * vf, axis=1, keepdims=True) + 1e-06)
    h = jnp.concatenate(hs, axis=1) * vgain[...]
    v_inner = jnp.mean(h * vf, axis=1, keepdims=True)
    vg_out[...] = (vscale * h - vf * vscale * vscale * vscale * v_inner).astype(BF16)

    @pl.loop(1, dp)
    def _(k):
        block = r4.at[:, dprev(k)]
        remote(block, block, b2_s.at[k], b2_r.at[k], (me_d, partner)).wait_recv()

    kvs_out[...] = r4[...]

    for copy in sends:
        copy.wait_send()

    @pl.loop(1, dp)
    def _(k):
        a1(k, 0).wait_send()
        a1(k, 1).wait_send()
        a2(k, 0).wait_send()
        a2(k, 1).wait_send()
        b1(k).wait_send()
        b2(k).wait_send()

    @pl.loop(0, width // step)
    def _(j):
        text_copy(j).wait()


def shards(vision, vision_gain, image_slot, text_embed, w_proj, llm_gain, w_key, w_value, key_grad, value_grad):
    dp = lax.axis_size("dp")
    mp = lax.axis_size("mp")
    here = lax.axis_index("dp")
    tokens, width = text_embed.shape
    slots = tokens // PATCH
    rows, dv = vision.shape
    kvd = key_grad.shape[1]
    kv = kvd * mp
    img = rows * mp
    rb = PATCH // dp
    ys = mp // 2
    pieces = 5 if dv % 640 == 0 else 1
    span = dv // pieces
    slot_ids = jnp.arange(dp * slots, dtype=jnp.int32)
    hot = slot_ids[:, None] == image_slot[None, :]
    owner = jnp.sum(jnp.where(hot, jnp.arange(dp, dtype=jnp.int32)[None, :], 0), axis=1).astype(jnp.int32)
    V = pltpu.VMEM
    any_spec = pl.BlockSpec(memory_space=pl.ANY)
    vmem = pl.BlockSpec(memory_space=pltpu.VMEM)
    smem = pl.BlockSpec(memory_space=pltpu.SMEM)
    scratch = [
        V((rows, dv), BF16), V((mp, rows, dv), BF16), V((tokens, width), BF16), V((dv, width), BF16),
        V((width, kv), BF16), V((width, kv), BF16), V((tokens, width), BF16),
        V((tokens, kv), BF16), V((tokens, kv), BF16), V((img, kv), BF16), V((img, kv), BF16),
        V((img, width), BF16), V((img, width), BF16), V((img, width), BF16), V((img, width), F32),
    ]
    for n in (tokens, img):
        scratch += [
            V((ys, n, 2 * kvd), BF16), V((ys, n, 2 * kvd), F32), V((ys, n, 2 * kvd), BF16),
            V((ys, n, 2 * kvd), BF16), V((ys, n, 2 * kvd), BF16),
        ]
    scratch += [
        V((pieces, ys, rows, span), BF16), V((pieces, ys, rows, span), F32), V((pieces, ys, rows, span), BF16),
        V((pieces, ys, rows, span), BF16), V((pieces, ys, rows, span), BF16),
        V((tokens, 2 * kvd), F32), V((img, 2 * kvd), F32),
        V((8, tokens), F32), V((mp, 8, tokens), F32), V((8, img), F32), V((mp, 8, img), F32),
        V((tokens, 128), F32), V((tokens, 128), F32), V((img, 128), F32), V((img, 128), F32),
        V((dp * slots, rb, kvd), BF16), V((dp * slots, rb, kvd), BF16),
        V((dp, rb, kvd), BF16), V((dp, rb, kvd), BF16), V((dp, rb, kvd), BF16), V((dp, rb, kvd), BF16),
        V((dp, rb, 2 * kvd), BF16), V((dp, rb, 2 * kvd), BF16),
        V((dp, slots, rb, 2 * kvd), BF16), V((slots, dp, rb, 2 * kvd), BF16),
        V((tokens, width), BF16),
        DMA((9,)), DMA((5, 2, ys)), DMA((5, 2, ys)), DMA((2, 2, ys)), DMA((2, 2, ys)),
        DMA((2, mp)), DMA((2, mp)), DMA((2, pieces, ys)), DMA((2, pieces, ys)),
        DMA((2, dp)), DMA((2, dp)), DMA((2, dp)), DMA((2, dp)),
        DMA((dp,)), DMA((dp,)), DMA((dp,)), DMA((dp,)), DMA((width // 256,)),
    ]
    kvt, kvs, tg, vgrad = pl.pallas_call(
        functools.partial(kernel, dp, mp),
        out_shape=(
            jax.ShapeDtypeStruct((tokens, 2 * kvd), BF16),
            jax.ShapeDtypeStruct((slots, dp, rb, 2 * kvd), BF16),
            jax.ShapeDtypeStruct((tokens, width), BF16),
            jax.ShapeDtypeStruct((rows, dv), BF16),
        ),
        in_specs=[smem, smem, any_spec, vmem, any_spec, any_spec, vmem] + [any_spec] * 6,
        out_specs=(vmem, vmem, any_spec, vmem),
        scratch_shapes=scratch,
        compiler_params=pltpu.CompilerParams(
            collective_id=0, has_side_effects=True, vmem_limit_bytes=67043328
        ),
    )(
        image_slot, owner, vision, vision_gain[None, :], text_embed, w_proj, llm_gain[None, :],
        w_key, w_value, key_grad, value_grad,
        key_grad.reshape(slots, dp, rb, kvd), value_grad.reshape(slots, dp, rb, kvd),
    )
    near = slot_ids.reshape(dp, slots)[here]
    filled = jnp.any(near[:, None] == image_slot[None, :], axis=1)
    filled = jnp.repeat(filled, PATCH)[:, None]
    kv_final = jnp.where(filled, kvs.reshape(tokens, 2 * kvd), kvt)
    text_grad = jnp.where(filled, jnp.zeros_like(tg), tg)
    return kv_final[:, :kvd], kv_final[:, kvd:], text_grad, vgrad


def solution(mesh):
    placed = (
        P(("dp", "mp"), None),
        P(),
        P(),
        P("dp", "mp"),
        P(None, "mp"),
        P("mp"),
        P("mp", None),
        P("mp", None),
        P("dp", "mp"),
        P("dp", "mp"),
    )
    return jax.shard_map(
        shards,
        mesh=mesh,
        in_specs=placed,
        out_specs=(P("dp", "mp"), P("dp", "mp"), P("dp", "mp"), P(("dp", "mp"), None)),
        check_vma=False,
    )
```

time: 270 us -> 95.9 us (0.36)
  the two profiles are of different devices: /device:TPU:0 before, /device:TPU:24 now
where the time goes in v2:
time: 95.9 us; the launch traced here: 95.6 us
  Pallas kernels  84.8 us (88%)
  other arithmetic  6.6 us (7%)
  local copies, waits for them, and re-layouts  3.52 us (4%)
    pallas_call x1, Pallas kernels, shards(): pl.pallas_call(functools.partial(kernel, dp, mp), out_shape=(jax.ShapeDty...  84.8 us
    select_n x1, other arithmetic, shards(): text_grad = jnp.where(filled, jnp.zeros_like(tg), tg)  3.17 us

profile of v2, /device:TPU:24, one launch (start us, length us, event | category | flops | bytes accessed | tf_op | source)
XLA Modules:
  0.0 95.6 jit_solution(5372297864332083331)
XLA Ops:
  0.6 1.2 %select_reduce_fusion.owner_ref = s32[16]{0:T(128)} fusion(s32[8]{0:T(128)} %slot_ref.1), kind=kLoop, calls=%fused_computation.2 | loop fusion | flops 368 | bytes 96 | tf_op jit(solution)/shard_map/reduce_sum | solution.py:441
  1.9 0.8 compare_reduce_fusion
  2.7 0.1 broadcast_in_dim.46
  2.8 0.5 broadcast_in_dim.47
  3.3 1.3 %broadcast_in_dim.51.vgain = f32[1,3200]{1,0:T(1,128)} reshape(f32[3200]{0:T(1024)} %param.11) | data formatting | bytes 25600 | tf_op jit(solution)/shard_map/broadcast_in_dim | solution.py:488
  4.7 84.8 %shard_map.129 = (bf16[512,512]{1,0:T(8,128)(2,1)}, bf16[2,8,32,512]{3,2,1,0:T(8,128)(2,1)}, bf16[512,2048]{1,0:T(8,128)(2,1)}, bf16[64,3200]{1,0:T(8,128)(2,1)}) custom-call(s32[8]{0:T(128)} %slot_ref.1, s32[16]{0:T(128)} %select_reduce_fusion.owner_ref, bf16[64,3200]{1,0:T(8,128)(2,1)} %vision_h.1, f32[1,3200]{1,0:T(1,128)} %broadcast_in_dim.51.vgain, ...), custom_call_target="tpu_custom_call" | custom-call | tf_op jit(solution)/shard_map/pallas_call | solution.py:473
  89.5 1.3 %bitcast_select_fusion = bf16[512,512]{1,0:T(8,128)(2,1)S(1)} fusion(bf16[512,512]{1,0:T(8,128)(2,1)} %get-tuple-element.9, bf16[2,8,32,512]{3,2,1,0:T(8,128)(2,1)} %get-tuple-element.8, pred[512]{0:T(512)(128)(4,1)} %broadcast_in_dim.47), kind=kLoop, calls=%fused_computation.1 | loop fusion | flops 262144 | bytes 1573376 | tf_op jit(solution)/shard_map/jit(_where)/select_n | solution.py:495
  90.9 0.0 copy-start
  90.9 3.2 %broadcast_select_fusion = bf16[512,2048]{1,0:T(8,128)(2,1)} fusion(bf16[512,2048]{1,0:T(8,128)(2,1)} %get-tuple-element.10, pred[512]{0:T(512)(128)(4,1)} %broadcast_in_dim.47), kind=kLoop, calls=%fused_computation | loop fusion | flops 1048576 | bytes 4194816 | tf_op jit(solution)/shard_map/jit(_where)/select_n | solution.py:496
  94.0 0.8 fusion
  94.9 0.0 copy-done
  94.9 0.8 copy.15
  (2 shorter events, 0.0 us)
Async XLA Ops:
  90.9 4.0 %copy-start = (bf16[64,3200]{1,0:T(8,128)(2,1)S(1)}, bf16[64,3200]{1,0:T(8,128)(2,1)}, u32[]{:S(2)}) copy-start(bf16[64,3200]{1,0:T(8,128)(2,1)} %get-tuple-element.21) | copy-start | bytes 1228804

commit v3 on v2

--- a/solution.py
+++ b/solution.py
@@ -37,8 +37,8 @@
 
 
 def kernel(
-    dp, mp, slot_ref, owner_ref, vision_h, vgain, text_h, wp_h, gain, wk_h, wv_h, kg_h, vg_h, kg4, vg4,
-    kvt_out, kvs_out, tg_h, vg_out,
+    dp, mp, slot_ref, vision_h, vgain, text_h, wp_h, gain, wk_h, wv_h, kg_h, vg_h, kg4, vg4,
+    k_out, v_out, tg_h, vg_out,
     vis, vis_all, text, wp, wk, wv, xt, gk, gv, gik, giv, emb, xi, dimg, dg,
     t_send, t_own, t_l1, t_s2, t_l2, i_send, i_own, i_l1, i_s2, i_l2,
     d_send, d_own, d_l1, d_s2, d_l2, kvt, kvi,
@@ -76,6 +76,18 @@
     def col(m):
         return pl.ds(pl.multiple_of(m * kvd, kvd), kvd)
 
+    def owner_of(slot):
+        found = jnp.int32(0)
+        for i in range(dp):
+            found = jnp.where(slot_ref[i] == slot, jnp.int32(i), found)
+        return found
+
+    def filled(s):
+        found = jnp.int32(0)
+        for i in range(dp):
+            found = jnp.where(slot_ref[i] == me_d * slots + s, jnp.int32(1), found)
+        return found.astype(F32)
+
     sends = []
 
     def send(*args):
@@ -178,7 +190,10 @@
             yk = ynext(k)
             arrived(l1.at[yk], rs_s.at[n, 0, k], rs_r.at[n, 0, k])
             s2[k] = (own[yk] + l1[yk].astype(F32)).astype(BF16)
-            send(s2.at[k], l2.at[k], rs_s.at[n, 1, k], rs_r.at[n, 1, k], (me_d, yk * 2 + core))
+
+    def level_go(n, s2, l2):
+        for k in range(ycount - 1, 0, -1):
+            send(s2.at[k], l2.at[k], rs_s.at[n, 1, k], rs_r.at[n, 1, k], (me_d, ynext(k) * 2 + core))
 
     def level_end(n, own, l1, l2):
         arrived(l1.at[y], rs_s.at[n, 0, 0], rs_r.at[n, 0, 0])
@@ -192,15 +207,15 @@
         for k in range(1, mp):
             send(st, sr.at[k], st_s.at[n, k], st_r.at[n, k], (me_d, lax.rem(me + k, mp)))
 
-    def stats_end(n, st, sr, sc, co):
+    def stats_end(n, st, sr, sc, co, keep):
         total = st[...]
         for k in range(1, mp):
             arrived(sr.at[k], st_s.at[n, k], st_r.at[n, k])
             total = total + sr[k]
         sq, inner = to_columns(total)
         scale = lax.rsqrt(sq / d_model + 1e-05)
-        sc[...] = jnp.broadcast_to(scale, sc.shape)
-        co[...] = jnp.broadcast_to(scale * scale * scale * (inner / d_model), co.shape)
+        sc[...] = jnp.broadcast_to(scale * keep, sc.shape)
+        co[...] = jnp.broadcast_to(scale * scale * scale * (inner / d_model) * keep, co.shape)
 
     loads[3].wait()
     tf = text[...].astype(F32)
@@ -212,34 +227,6 @@
     gather_relay(0, vis_block)
     level_two(0, t_own, t_l1, t_s2, t_l2)
 
-    loads[7].wait()
-    loads[8].wait()
-
-    @pl.loop(1, dp)
-    def _(k):
-        for which, dst in ((0, r1k), (1, r1v)):
-            block = dst.at[pl.ds(dprev(k) * slots, slots)]
-            remote(block, block, a1_s.at[which, k], a1_r.at[which, k], (me_d, partner)).wait_recv()
-
-    @pl.loop(0, dp)
-    def _(i):
-        s2k[i] = r1k[slot_ref[i]]
-        s2v[i] = r1v[slot_ref[i]]
-
-    r2k[me_d] = s2k[me_d]
-    r2v[me_d] = s2v[me_d]
-
-    def a2(k, which):
-        src, dst = ((s2k, r2k), (s2v, r2v))[which]
-        return remote(
-            src.at[dnext(k)], dst.at[me_d], a2_s.at[which, k], a2_r.at[which, k], (dnext(k), me)
-        )
-
-    @pl.loop(1, dp)
-    def _(k):
-        a2(k, 0).start()
-        a2(k, 1).start()
-
     gather_finish(0, vis_block)
     loads[6].wait()
     step = 256
@@ -255,11 +242,41 @@
         xi[:, cs] = (ef * gain[:, cs]).astype(BF16)
         return acc + jnp.sum(ef * ef, axis=1, keepdims=True)
 
-    sq_i = lax.fori_loop(0, width // step, project, jnp.zeros((dimg_rows, 1), F32))
+    half = width // step // 2
+    sq_i = lax.fori_loop(0, half, project, jnp.zeros((dimg_rows, 1), F32))
+
+    loads[7].wait()
+    loads[8].wait()
+
+    @pl.loop(1, dp)
+    def _(k):
+        for which, dst in ((0, r1k), (1, r1v)):
+            block = dst.at[pl.ds(dprev(k) * slots, slots)]
+            remote(block, block, a1_s.at[which, k], a1_r.at[which, k], (me_d, partner)).wait_recv()
+
+    @pl.loop(0, dp)
+    def _(i):
+        s2k[i] = r1k[slot_ref[i]]
+        s2v[i] = r1v[slot_ref[i]]
+
+    r2k[me_d] = s2k[me_d]
+    r2v[me_d] = s2v[me_d]
+
+    def a2(k, which):
+        src, dst = ((s2k, r2k), (s2v, r2v))[which]
+        return remote(
+            src.at[dnext(k)], dst.at[me_d], a2_s.at[which, k], a2_r.at[which, k], (dnext(k), me)
+        )
+
+    @pl.loop(1, dp)
+    def _(k):
+        a2(k, 0).start()
+        a2(k, 1).start()
+
+    sq_i = lax.fori_loop(half, width // step, project, sq_i)
     stage(xi, 1, i_send, i_own, i_l1)
-    gather_relay(1, gk_block)
-    gather_relay(2, gv_block)
     level_two(1, i_own, i_l1, i_s2, i_l2)
+    level_go(1, i_s2, i_l2)
 
     @pl.loop(1, dp)
     def _(k):
@@ -273,33 +290,9 @@
     giv[:, col(me)] = own_v.astype(BF16)
     gather_start(3, gik_block)
     gather_start(4, giv_block)
-
-    total = level_end(0, t_own, t_l1, t_l2)
-    kvt[...] = total
-    inner = jnp.sum(
-        total[:, :kvd] * gk[:, col(me)].astype(F32) + total[:, kvd:] * gv[:, col(me)].astype(F32),
-        axis=1, keepdims=True,
-    )
-    st_t[...] = to_rows(sq_t, inner)
-    stats_send(0, st_t, sr_t)
-    gather_finish(1, gk_block)
-    gather_finish(2, gv_block)
-    stats_end(0, st_t, sr_t, sc_t, co_t)
-    kvt_out[...] = (kvt[...] * sc_t[:, 0:1]).astype(BF16)
-
-    def text_copy(j):
-        cs = pl.ds(pl.multiple_of(j * step, step), step)
-        return pltpu.make_async_copy(tg.at[:, cs], tg_h.at[:, cs], tg_sem.at[j])
-
-    def text_back(j, _):
-        cs = pl.ds(pl.multiple_of(j * step, step), step)
-        d = nt(gk[...], wk[cs, :]) + nt(gv[...], wv[cs, :])
-        d = sc_t[:, 0:1] * (d * gain[:, cs]) - text[:, cs].astype(F32) * co_t[:, 0:1]
-        tg[:, cs] = d.astype(BF16)
-        text_copy(j).start()
-        return 0
-
-    lax.fori_loop(0, width // step, text_back, 0)
+    level_go(0, t_s2, t_l2)
+    gather_relay(1, gk_block)
+    gather_relay(2, gv_block)
 
     total = level_end(1, i_own, i_l1, i_l2)
     kvi[...] = total
@@ -320,7 +313,7 @@
         return 0
 
     lax.fori_loop(0, width // step, image_back, 0)
-    stats_end(1, st_i, sr_i, sc_i, co_i)
+    stats_end(1, st_i, sr_i, sc_i, co_i, 1.0)
     kvb[...] = (kvi[...] * sc_i[:, 0:1]).reshape(dp, rb, 2 * kvd).astype(BF16)
     r3[me_d] = kvb[me_d]
 
@@ -375,7 +368,7 @@
             @pl.loop(0, dp)
             def _(d):
                 for s in range(slots):
-                    s4[d, s] = r3[owner_ref[d * slots + s]]
+                    s4[d, s] = r3[owner_of(d * slots + s)]
 
             for s in range(slots):
                 r4[s, me_d] = s4[me_d, s]
@@ -385,6 +378,34 @@
                 b2(k).start()
 
     vis_two(pieces - 1)
+
+    total = level_end(0, t_own, t_l1, t_l2)
+    kvt[...] = total
+    inner = jnp.sum(
+        total[:, :kvd] * gk[:, col(me)].astype(F32) + total[:, kvd:] * gv[:, col(me)].astype(F32),
+        axis=1, keepdims=True,
+    )
+    st_t[...] = to_rows(sq_t, inner)
+    stats_send(0, st_t, sr_t)
+    gather_finish(1, gk_block)
+    gather_finish(2, gv_block)
+    keep = jnp.concatenate([jnp.full((PATCH, 1), 1.0, F32) * (1.0 - filled(s)) for s in range(slots)], axis=0)
+    stats_end(0, st_t, sr_t, sc_t, co_t, keep)
+
+    def text_copy(j):
+        cs = pl.ds(pl.multiple_of(j * step, step), step)
+        return pltpu.make_async_copy(tg.at[:, cs], tg_h.at[:, cs], tg_sem.at[j])
+
+    def text_back(j, _):
+        cs = pl.ds(pl.multiple_of(j * step, step), step)
+        d = nt(gk[...], wk[cs, :]) + nt(gv[...], wv[cs, :])
+        d = sc_t[:, 0:1] * (d * gain[:, cs]) - text[:, cs].astype(F32) * co_t[:, 0:1]
+        tg[:, cs] = d.astype(BF16)
+        text_copy(j).start()
+        return 0
+
+    lax.fori_loop(0, width // step, text_back, 0)
+
     hs = []
     for j in range(pieces):
         d = d_own[j, y] + d_l1[j, y].astype(F32)
@@ -403,7 +424,11 @@
         block = r4.at[:, dprev(k)]
         remote(block, block, b2_s.at[k], b2_r.at[k], (me_d, partner)).wait_recv()
 
-    kvs_out[...] = r4[...]
+    for s in range(slots):
+        at = pl.ds(s * PATCH, PATCH)
+        out = kvt[at, :] * sc_t[at, 0:1] + r4[s].astype(F32).reshape(PATCH, 2 * kvd) * filled(s)
+        k_out[at, :] = out[:, :kvd].astype(BF16)
+        v_out[at, :] = out[:, kvd:].astype(BF16)
 
     for copy in sends:
         copy.wait_send()
@@ -425,7 +450,6 @@
 def shards(vision, vision_gain, image_slot, text_embed, w_proj, llm_gain, w_key, w_value, key_grad, value_grad):
     dp = lax.axis_size("dp")
     mp = lax.axis_size("mp")
-    here = lax.axis_index("dp")
     tokens, width = text_embed.shape
     slots = tokens // PATCH
     rows, dv = vision.shape
@@ -436,9 +460,6 @@
     ys = mp // 2
     pieces = 5 if dv % 640 == 0 else 1
     span = dv // pieces
-    slot_ids = jnp.arange(dp * slots, dtype=jnp.int32)
-    hot = slot_ids[:, None] == image_slot[None, :]
-    owner = jnp.sum(jnp.where(hot, jnp.arange(dp, dtype=jnp.int32)[None, :], 0), axis=1).astype(jnp.int32)
     V = pltpu.VMEM
     any_spec = pl.BlockSpec(memory_space=pl.ANY)
     vmem = pl.BlockSpec(memory_space=pltpu.VMEM)
@@ -470,31 +491,25 @@
         DMA((2, dp)), DMA((2, dp)), DMA((2, dp)), DMA((2, dp)),
         DMA((dp,)), DMA((dp,)), DMA((dp,)), DMA((dp,)), DMA((width // 256,)),
     ]
-    kvt, kvs, tg, vgrad = pl.pallas_call(
+    return pl.pallas_call(
         functools.partial(kernel, dp, mp),
         out_shape=(
-            jax.ShapeDtypeStruct((tokens, 2 * kvd), BF16),
-            jax.ShapeDtypeStruct((slots, dp, rb, 2 * kvd), BF16),
+            jax.ShapeDtypeStruct((tokens, kvd), BF16),
+            jax.ShapeDtypeStruct((tokens, kvd), BF16),
             jax.ShapeDtypeStruct((tokens, width), BF16),
             jax.ShapeDtypeStruct((rows, dv), BF16),
         ),
-        in_specs=[smem, smem, any_spec, vmem, any_spec, any_spec, vmem] + [any_spec] * 6,
+        in_specs=[smem, any_spec, vmem, any_spec, any_spec, vmem] + [any_spec] * 6,
         out_specs=(vmem, vmem, any_spec, vmem),
         scratch_shapes=scratch,
         compiler_params=pltpu.CompilerParams(
             collective_id=0, has_side_effects=True, vmem_limit_bytes=67043328
         ),
     )(
-        image_slot, owner, vision, vision_gain[None, :], text_embed, w_proj, llm_gain[None, :],
+        image_slot, vision, vision_gain[None, :], text_embed, w_proj, llm_gain[None, :],
         w_key, w_value, key_grad, value_grad,
         key_grad.reshape(slots, dp, rb, kvd), value_grad.reshape(slots, dp, rb, kvd),
     )
-    near = slot_ids.reshape(dp, slots)[here]
-    filled = jnp.any(near[:, None] == image_slot[None, :], axis=1)
-    filled = jnp.repeat(filled, PATCH)[:, None]
-    kv_final = jnp.where(filled, kvs.reshape(tokens, 2 * kvd), kvt)
-    text_grad = jnp.where(filled, jnp.zeros_like(tg), tg)
-    return kv_final[:, :kvd], kv_final[:, kvd:], text_grad, vgrad
 
 
 def solution(mesh):

time: 95.9 us -> 89 us (0.928)
  the two profiles are of different devices: /device:TPU:24 before, /device:TPU:0 now
where the time goes in v3:
time: 89 us; the launch traced here: 88.7 us
  Pallas kernels  79.4 us (89%)
  local copies, waits for them, and re-layouts  8.63 us (10%)
    pallas_call x1, Pallas kernels, shards(): pl.pallas_call(functools.partial(kernel, dp, mp), out_shape=(jax.ShapeDty...  79.4 us
    unnamed x6, local copies, waits for them, and re-layouts  7.3 us

profile of v3, /device:TPU:0, one launch (start us, length us, event | category | flops | bytes accessed | tf_op | source)
XLA Modules:
  0.0 88.7 jit_solution(4149255108145514834)
XLA Ops:
  0.6 1.3 %broadcast_in_dim.6.vgain = f32[1,3200]{1,0:T(1,128)} reshape(f32[3200]{0:T(1024)} %param.11) | data formatting | bytes 25600 | tf_op jit(solution)/shard_map/broadcast_in_dim | solution.py:509
  2.0 79.4 %shard_map.129 = (bf16[512,256]{1,0:T(8,128)(2,1)}, bf16[512,256]{1,0:T(8,128)(2,1)}, bf16[512,2048]{1,0:T(8,128)(2,1)}, bf16[64,3200]{1,0:T(8,128)(2,1)}) custom-call(s32[8]{0:T(128)} %slot_ref.1, bf16[64,3200]{1,0:T(8,128)(2,1)} %vision_h.1, f32[1,3200]{1,0:T(1,128)} %broadcast_in_dim.6.vgain, bf16[512,2048]{1,0:T(8,128)(2,1)} %text_h.1, ...), custom_call_target="tpu_custom_call" | custom-call | tf_op jit(solution)/shard_map/pallas_call | solution.py:494
  81.3 0.0 copy-start
  81.4 1.7 %copy.18 = bf16[512,256]{1,0:T(8,128)(2,1)} copy(bf16[512,256]{1,0:T(8,128)(2,1)} %get-tuple-element.8) | data formatting | bytes 524288
  83.1 1.7 %copy.19 = bf16[512,256]{1,0:T(8,128)(2,1)} copy(bf16[512,256]{1,0:T(8,128)(2,1)} %get-tuple-element.9) | data formatting | bytes 524288
  84.7 3.2 %copy.20 = bf16[512,2048]{1,0:T(8,128)(2,1)} copy(bf16[512,2048]{1,0:T(8,128)(2,1)} %get-tuple-element.10) | data formatting | bytes 4194304
  87.9 0.0 copy-done
  87.9 0.8 copy.21
Async XLA Ops:
  81.3 6.6 %copy-start = (bf16[64,3200]{1,0:T(8,128)(2,1)S(1)}, bf16[64,3200]{1,0:T(8,128)(2,1)}, u32[]{:S(2)}) copy-start(bf16[64,3200]{1,0:T(8,128)(2,1)} %get-tuple-element.11) | copy-start | bytes 1228804

commit v4 on v3

--- a/solution.py
+++ b/solution.py
@@ -45,7 +45,7 @@
     st_t, sr_t, st_i, sr_i, sc_t, co_t, sc_i, co_i,
     r1k, r1v, s2k, s2v, r2k, r2v, kvb, r3, s4, r4, tg,
     load_sem, ag_s, ag_r, rs_s, rs_r, st_s, st_r, dv_s, dv_r,
-    a1_s, a1_r, a2_s, a2_r, b1_s, b1_r, b2_s, b2_r, tg_sem,
+    a1_s, a1_r, a2_s, a2_r, b1_s, b1_r, b2_s, b2_r, tg_sem, dt,
 ):
     me_d = lax.axis_index("dp")
     me = lax.axis_index("mp")
@@ -293,6 +293,15 @@
     level_go(0, t_s2, t_l2)
     gather_relay(1, gk_block)
     gather_relay(2, gv_block)
+    gather_finish(1, gk_block)
+    gather_finish(2, gv_block)
+
+    def text_product(j, _):
+        cs = pl.ds(pl.multiple_of(j * step, step), step)
+        dt[:, cs] = (nt(gk[...], wk[cs, :]) + nt(gv[...], wv[cs, :])) * gain[:, cs]
+        return 0
+
+    lax.fori_loop(0, width // step, text_product, 0)
 
     total = level_end(1, i_own, i_l1, i_l2)
     kvi[...] = total
@@ -387,8 +396,6 @@
     )
     st_t[...] = to_rows(sq_t, inner)
     stats_send(0, st_t, sr_t)
-    gather_finish(1, gk_block)
-    gather_finish(2, gv_block)
     keep = jnp.concatenate([jnp.full((PATCH, 1), 1.0, F32) * (1.0 - filled(s)) for s in range(slots)], axis=0)
     stats_end(0, st_t, sr_t, sc_t, co_t, keep)
 
@@ -398,8 +405,7 @@
 
     def text_back(j, _):
         cs = pl.ds(pl.multiple_of(j * step, step), step)
-        d = nt(gk[...], wk[cs, :]) + nt(gv[...], wv[cs, :])
-        d = sc_t[:, 0:1] * (d * gain[:, cs]) - text[:, cs].astype(F32) * co_t[:, 0:1]
+        d = sc_t[:, 0:1] * dt[:, cs] - text[:, cs].astype(F32) * co_t[:, 0:1]
         tg[:, cs] = d.astype(BF16)
         text_copy(j).start()
         return 0
@@ -489,7 +495,7 @@
         DMA((9,)), DMA((5, 2, ys)), DMA((5, 2, ys)), DMA((2, 2, ys)), DMA((2, 2, ys)),
         DMA((2, mp)), DMA((2, mp)), DMA((2, pieces, ys)), DMA((2, pieces, ys)),
         DMA((2, dp)), DMA((2, dp)), DMA((2, dp)), DMA((2, dp)),
-        DMA((dp,)), DMA((dp,)), DMA((dp,)), DMA((dp,)), DMA((width // 256,)),
+        DMA((dp,)), DMA((dp,)), DMA((dp,)), DMA((dp,)), DMA((width // 256,)), V((tokens, width), F32),
     ]
     return pl.pallas_call(
         functools.partial(kernel, dp, mp),

time: 89 us -> 84.8 us (0.953)
  Pallas kernels: 79.4 us -> 75.2 us
    pallas_call x1, Pallas kernels: 79.4 us -> 75.2 us  [shards(): pl.pallas_call(functools.partial(kernel, dp, mp), out_shape=(jax.ShapeDty...]
where the time goes in v4:
time: 84.8 us; the launch traced here: 84.5 us
  Pallas kernels  75.2 us (89%)
  local copies, waits for them, and re-layouts  8.63 us (10%)
    pallas_call x1, Pallas kernels, shards(): pl.pallas_call(functools.partial(kernel, dp, mp), out_shape=(jax.ShapeDty...  75.2 us
    unnamed x6, local copies, waits for them, and re-layouts  7.3 us

profile of v4, /device:TPU:0, one launch (start us, length us, event | category | flops | bytes accessed | tf_op | source)
XLA Modules:
  0.0 84.5 jit_solution(161730307703553798)
XLA Ops:
  0.6 1.3 %broadcast_in_dim.6.vgain = f32[1,3200]{1,0:T(1,128)} reshape(f32[3200]{0:T(1024)} %param.11) | data formatting | bytes 25600 | tf_op jit(solution)/shard_map/broadcast_in_dim | solution.py:515
  2.0 75.2 %shard_map.129 = (bf16[512,256]{1,0:T(8,128)(2,1)}, bf16[512,256]{1,0:T(8,128)(2,1)}, bf16[512,2048]{1,0:T(8,128)(2,1)}, bf16[64,3200]{1,0:T(8,128)(2,1)}) custom-call(s32[8]{0:T(128)} %slot_ref.1, bf16[64,3200]{1,0:T(8,128)(2,1)} %vision_h.1, f32[1,3200]{1,0:T(1,128)} %broadcast_in_dim.6.vgain, bf16[512,2048]{1,0:T(8,128)(2,1)} %text_h.1, ...), custom_call_target="tpu_custom_call" | custom-call | tf_op jit(solution)/shard_map/pallas_call | solution.py:500
  77.1 0.0 copy-start
  77.2 1.7 %copy.18 = bf16[512,256]{1,0:T(8,128)(2,1)} copy(bf16[512,256]{1,0:T(8,128)(2,1)} %get-tuple-element.8) | data formatting | bytes 524288
  78.9 1.7 %copy.19 = bf16[512,256]{1,0:T(8,128)(2,1)} copy(bf16[512,256]{1,0:T(8,128)(2,1)} %get-tuple-element.9) | data formatting | bytes 524288
  80.5 3.2 %copy.20 = bf16[512,2048]{1,0:T(8,128)(2,1)} copy(bf16[512,2048]{1,0:T(8,128)(2,1)} %get-tuple-element.10) | data formatting | bytes 4194304
  83.7 0.0 copy-done
  83.7 0.8 copy.21
Async XLA Ops:
  77.1 6.6 %copy-start = (bf16[64,3200]{1,0:T(8,128)(2,1)S(1)}, bf16[64,3200]{1,0:T(8,128)(2,1)}, u32[]{:S(2)}) copy-start(bf16[64,3200]{1,0:T(8,128)(2,1)} %get-tuple-element.11) | copy-start | bytes 1228804
